TPU v7x, 32 devices: a whole 2x2x4 slice. The times are simulated.
32 devices in a mesh: grp: 2 (over y), tp: 4 (over z), dp: 2 (over x), sub: 2 (over core).
Axes of the slice: x: 2, y: 2, z: 4, core: 2. Of those that a mesh axis runs over, the one named last changes fastest.
Arguments:
- hidden_in: bfloat16 [240, 26624], P(('grp', 'dp', 'sub'), 'tp'), parts along dimension 0, may hold values from -6 to 6
- out_grad: bfloat16 [240, 8192], P(('grp', 'tp'), ('dp', 'sub')), parts along dimension 0, may hold values from -6 to 6
- base_levels: bfloat16 [26624, 8192], P('tp', ('dp', 'sub')), may hold values from -1 to 1, as said below
- base_scales: bfloat16 [416, 8192], P('tp', ('dp', 'sub')), may hold values from 0.0079956055 to 0.015991211
- kron_outer: float32 [4, 4], P('tp', ('dp', 'sub')), may hold values from -3 to 3
- kron_left: bfloat16 [6656, 16], replicated, may hold values from -0.078125 to 0.078125
- kron_right: bfloat16 [16, 2048], replicated, may hold values from -0.125 to 0.125
- sparse_rows: int32 [4, 4, 8], P('tp', ('dp', 'sub')), may hold values from 0 to 51, as said below
- sparse_cols: int32 [4, 4, 8], P('tp', ('dp', 'sub')), may hold values from 0 to 15, as said below
- sparse_count: int32 [4, 4], P('tp', ('dp', 'sub')), may hold values from 1 to 8, as said below
- sparse_values: bfloat16 [4, 4, 8, 128, 128], P('tp', ('dp', 'sub')), may hold values from -0.3125 to 0.3125
Outputs:
- layer_out: bfloat16 [240, 8192], P(('grp', 'tp'), ('dp', 'sub')), parts along dimension 0
- input_grad: bfloat16 [240, 26624], P(('grp', 'dp', 'sub'), 'tp'), parts along dimension 0
- grad_outer: float32 [8, 4], P(('grp', 'tp'), ('dp', 'sub')), parts along dimension 0
- grad_left: float32 [13312, 16], P('grp'), parts along dimension 0
- grad_right: float32 [32, 2048], P('grp'), parts along dimension 0
- grad_sparse: float32 [8, 4, 8, 128, 128], P(('grp', 'tp'), ('dp', 'sub')), parts along dimension 0
There are 2 independent parts, one for each index of `grp`. A program takes and returns all parts, laid end to end along the dimension named above; an argument that names none is the same for every part. Nothing has to cross between parts.
Inputs may be any that keep to these rules, and one draw needn't show every extreme that they name: `base_levels`: every entry is one of the 16 levels of the NF4 code. `sparse_rows`: the 8 slots of a tile name distinct blocks, with sparse_cols. `sparse_cols`: the 8 slots of a tile name distinct blocks, with sparse_rows. `sparse_count`: slots at or past the count are unused; some tile uses all 8.
All inputs are finite; a program needn't handle non-finite values.
Results may differ from a plain program's by a relative error of at most 0.014.
Values may be sent and summed in bfloat16 or wider, within the bound.
A program may use at most 320 MiB of HBM per device.

v0:
```python
import functools

import jax
import jax.numpy as jnp
from jax import lax
from jax.experimental import pallas as pl
from jax.experimental.pallas import tpu as pltpu
from jax.sharding import PartitionSpec as P

F32 = jnp.float32
BF16 = jnp.bfloat16


def dot(a, b, ca, cb):
    return lax.dot_general(a, b, (((ca,), (cb,)), ((), ())), preferred_element_type=F32)


def pick_rows(tile_rows, tile_cols, block, quant):
    blocks = tile_rows // block
    best = tile_rows
    for n in range(1, blocks):
        if blocks % n == 0 and n * block * tile_cols <= 1 << 20 and n * block % (8 * quant) == 0:
            best = n * block
    return tile_rows if tile_rows * tile_cols <= 1 << 20 else best


def kernel(
    tokens, step_rows,
    slot_ref, rows_ref, cols_ref, count_ref, coef_ref,
    x_ref, dy_ref, kl_ref, kr_ref, sc_ref, val_ref, w_hbm,
    out_ref, ig_ref, go_ref, gl_ref, gr_ref, gs_ref,
    wbuf, wdq, acc, scf, vals, wsem,
):
    tile_rows, tile_cols = w_hbm.shape
    slots, block = val_ref.shape[0], val_ref.shape[1]
    col_blocks = tile_cols // block
    step_blocks = step_rows // block
    steps = tile_rows // step_rows
    quant = tile_rows // sc_ref.shape[0]
    inv = 1.0 / tokens
    coef = coef_ref[0, 0]

    def fetch(i, slot):
        return pltpu.make_async_copy(
            w_hbm.at[pl.ds(i * step_rows, step_rows)], wbuf.at[slot], wsem.at[slot]
        )

    fetch(0, 0).start()
    scf[...] = sc_ref[...].astype(F32)
    vals[pl.ds(0, slots)] = val_ref[...]
    vals[slots] = jnp.zeros((block, block), BF16)

    proj = dot(x_ref[...], kl_ref[...], 1, 0).astype(BF16)
    gproj = dot(dy_ref[...], kr_ref[...], 1, 1).astype(BF16)
    go_ref[...] = (jnp.sum(proj.astype(F32) * gproj.astype(F32)) * inv).reshape(1, 1)
    gl_ref[...] = dot(gproj, x_ref[...], 0, 0) * (coef * inv)
    gr_ref[...] = dot(proj, dy_ref[...], 0, 0) * (coef * inv)
    acc[...] = coef * dot(proj, kr_ref[...], 1, 0)

    @pl.loop(0, slots)
    def _(m):
        xr = x_ref[:, pl.ds(pl.multiple_of(rows_ref[m] * block, block), block)]
        dc = dy_ref[:, pl.ds(pl.multiple_of(cols_ref[m] * block, block), block)]
        live = jnp.where(m < count_ref[0, 0], inv, 0.0)
        gs_ref[m] = dot(xr, dc, 0, 0) * live

    @pl.loop(0, steps)
    def _(i):
        slot = lax.rem(i, 2)

        @pl.when(i + 1 < steps)
        def _():
            fetch(i + 1, 1 - slot).start()

        fetch(i, slot).wait()
        groups = step_rows // quant
        if steps == 1:
            scales = scf[...]
        else:
            scales = scf[pl.ds(pl.multiple_of(i * groups, 8), groups), :]
        for rb in range(step_blocks):
            for cb in range(col_blocks):
                delta = vals[slot_ref[(i * step_blocks + rb) * col_blocks + cb]]
                for q in range(block // quant):
                    r0 = rb * block + q * quant
                    lv = wbuf[slot, r0:r0 + quant, cb * block:(cb + 1) * block]
                    s = scales[r0 // quant:r0 // quant + 1, cb * block:(cb + 1) * block]
                    s16 = jnp.broadcast_to(s, (16, block)).astype(BF16)
                    w = lv.reshape(quant // 16, 16, block) * s16[None]
                    w = w.reshape(quant, block) + delta[q * quant:(q + 1) * quant]
                    wdq[r0:r0 + quant, cb * block:(cb + 1) * block] = w
        cols = pl.ds(pl.multiple_of(i * step_rows, block), step_rows)
        acc[...] += dot(x_ref[:, cols], wdq[...], 1, 0)
        back = dot(dy_ref[...], wdq[...], 1, 1)
        back += coef * dot(gproj, kl_ref[pl.ds(pl.multiple_of(i * step_rows, block), step_rows), :], 1, 1)
        ig_ref[:, cols] = back.astype(BF16)

    out_ref[...] = acc[...].astype(BF16)


def shards(
    hidden_in, out_grad, base_levels, base_scales, kron_outer, kron_left, kron_right,
    sparse_rows, sparse_cols, sparse_count, sparse_values,
):
    tile_rows, tile_cols = base_levels.shape
    slots, block = sparse_values.shape[2], sparse_values.shape[3]
    own = hidden_in.shape[0]
    pad = -own % 16
    rank = kron_left.shape[1]
    row_blocks, col_blocks = tile_rows // block, tile_cols // block
    n_s = lax.axis_size("dp") * lax.axis_size("sub")
    n_t = lax.axis_size("tp")
    tokens = own * n_s
    rows, cols = sparse_rows[0, 0], sparse_cols[0, 0]
    live = jnp.arange(slots) < sparse_count[0, 0]
    hit = ((rows * col_blocks + cols)[:, None] == jnp.arange(row_blocks * col_blocks)[None]) & live[:, None]
    slot_map = slots + jnp.sum(jnp.where(hit, jnp.arange(slots)[:, None] - slots, 0), axis=0)

    x = lax.all_gather(jnp.pad(hidden_in, ((0, pad), (0, 0))), ("dp", "sub"), axis=0, tiled=True)
    dy = lax.all_gather(jnp.pad(out_grad, ((0, pad), (0, 0))), "tp", axis=0, tiled=True)
    full = x.shape[0]
    step_rows = pick_rows(tile_rows, tile_cols, block, tile_rows // base_scales.shape[0])
    vmem = pl.BlockSpec(memory_space=pltpu.VMEM)
    smem = pl.BlockSpec(memory_space=pltpu.SMEM)
    out, ig, go, gl, gr, gs = pl.pallas_call(
        functools.partial(kernel, tokens, step_rows),
        in_specs=[smem] * 5 + [vmem] * 6 + [pl.BlockSpec(memory_space=pl.ANY)],
        out_specs=[vmem] * 6,
        out_shape=[
            jax.ShapeDtypeStruct((full, tile_cols), BF16),
            jax.ShapeDtypeStruct((full, tile_rows), BF16),
            jax.ShapeDtypeStruct((1, 1), F32),
            jax.ShapeDtypeStruct((rank, tile_rows), F32),
            jax.ShapeDtypeStruct((rank, tile_cols), F32),
            jax.ShapeDtypeStruct((slots, block, block), F32),
        ],
        scratch_shapes=[
            pltpu.VMEM((2, step_rows, tile_cols), BF16),
            pltpu.VMEM((step_rows, tile_cols), BF16),
            pltpu.VMEM((full, tile_cols), F32),
            pltpu.VMEM(base_scales.shape, F32),
            pltpu.VMEM((slots + 1, block, block), BF16),
            pltpu.SemaphoreType.DMA((2,)),
        ],
        compiler_params=pltpu.CompilerParams(vmem_limit_bytes=50 << 20),
    )(
        slot_map, rows, cols, sparse_count, kron_outer, x, dy, kron_left, kron_right,
        base_scales, sparse_values[0, 0], base_levels,
    )
    layer_out = lax.psum_scatter(out, "tp", scatter_dimension=0, tiled=True)[:own]
    input_grad = lax.psum_scatter(ig, ("dp", "sub"), scatter_dimension=0, tiled=True)[:own]
    gl, gr = lax.optimization_barrier(lax.psum(jnp.concatenate([gl, gr], 1), ("tp", "dp", "sub"))), None
    gl, gr = gl[:, :tile_rows], gl[:, tile_rows:]
    return layer_out, input_grad, go, gl.T, gr, gs[None, None]


def solution(mesh):
    return jax.shard_map(
        shards,
        mesh=mesh,
        in_specs=(
            P(("grp", "dp", "sub"), "tp"),
            P(("grp", "tp"), ("dp", "sub")),
            P("tp", ("dp", "sub")),
            P("tp", ("dp", "sub")),
            P("tp", ("dp", "sub")),
            P(),
            P(),
            P("tp", ("dp", "sub"), None),
            P("tp", ("dp", "sub"), None),
            P("tp", ("dp", "sub")),
            P("tp", ("dp", "sub"), None, None, None),
        ),
        out_specs=(
            P(("grp", "tp"), ("dp", "sub")),
            P(("grp", "dp", "sub"), "tp"),
            P(("grp", "tp"), ("dp", "sub")),
            P("grp", None),
            P("grp", None),
            P(("grp", "tp"), ("dp", "sub"), None, None, None),
        ),
        check_vma=False,
    )
```

profile of v0, /device:TPU:0, one launch (start us, length us, event | category | flops | bytes accessed | tf_op | source)
XLA Modules:
  0.0 216.6 jit_solution(13582002642205244287)
XLA Ops:
  7.2 0.0 copy-start.3
  7.2 0.0 copy-start.4
  7.2 0.0 all-gather.2.cloned.1.call-start
  7.2 1.8 pad.8
  9.0 0.0 all-gather.2.cloned.1.call-update
  9.1 0.0 all-reduce.4.cloned.1.call-start
  10.5 0.9 pad.9
  11.4 2.4 %copy.18.kl_ref = bf16[6656,16]{1,0:T(8,128)(2,1)} copy(bf16[6656,16]{0,1:T(8,128)(2,1)} %param.16) | data formatting | bytes 425984 | tf_op args[5]
  13.9 0.1 select_reduce_fusion
  13.9 17.4 %all_gather.7.dy_ref = bf16[128,2048]{1,0:T(8,128)(2,1)S(1)} all-gather(bf16[32,2048]{1,0:T(8,128)(2,1)S(1)} %pad.9), channel_id=1, replica_groups=mesh['grp'=2,'tp'=4,'dp'=2,'sub'=2] {'tp'}, dimensions={0}, use_global_device_ids=true | all-gather | bytes 655360 | tf_op jit(solution)/shard_map/all_gather | solution.py:120
  31.3 1.9 all-gather.2.cloned.1.call-done.x_ref
  33.3 0.0 copy-done.2
  33.3 29.9 %shard_map.154 = (bf16[128,2048]{1,0:T(8,128)(2,1)}, bf16[128,6656]{1,0:T(8,128)(2,1)}, f32[1,1]{1,0:T(1,128)}, f32[16,6656]{1,0:T(8,128)S(1)}, f32[16,2048]{1,0:T(8,128)S(1)}, /*index=5*/f32[8,128,128]{2,1,0:T(8,128)}) custom-call(s32[832]{0:T(1024)S(1)} %broadcast_add_fusion.slot_ref, s32[8]{0:T(128)S(1)} %bitcast.14, s32[8]{0:T(128)S(1)} %bitcast.13, ...), custom_call_target="tpu_custom_call" | custom-call | tf_op jit(solution)/shard_map/pallas_call | solution.py:125
  63.1 0.9 pad_maximum_fusion
  64.0 0.0 all-reduce.4.cloned.1.call-update
  64.0 0.0 reduce-scatter.3.cloned.1.call-start
  64.1 0.7 reduce-scatter.3.cloned.1.call-update
  64.7 0.0 reduce-scatter.5.cloned.1.call-start
  64.8 0.5 reduce-scatter.5.cloned.1.call-update
  65.3 90.1 %all-reduce.4.cloned.1.call-done = f32[16,8704]{1,0:T(8,128)} async-done(((f32[16,8704]{1,0:T(8,128)}), f32[16,8704]{1,0:T(8,128)}) %all-reduce.4.cloned.1.call-update) | async-done | bytes 557072 | tf_op jit(solution)/shard_map/psum | solution.py:152
  155.5 1.6 slice.19
  157.0 1.8 slice_bitcast_fusion
  158.8 21.2 %reduce-scatter.3.cloned.1.call-done = bf16[32,2048]{1,0:T(8,128)(2,1)} async-done(((bf16[128,2048]{1,0:T(8,128)(2,1)}), bf16[32,2048]{1,0:T(8,128)(2,1)}) %reduce-scatter.3.cloned.1.call-update) | async-done | bytes 131088 | tf_op jit(solution)/shard_map/reduce_scatter | solution.py:150
  180.0 30.1 %reduce-scatter.5.cloned.1.call-done = bf16[32,6656]{1,0:T(8,128)(2,1)} async-done(((bf16[128,6656]{1,0:T(8,128)(2,1)}), bf16[32,6656]{1,0:T(8,128)(2,1)}) %reduce-scatter.5.cloned.1.call-update) | async-done | bytes 426000 | tf_op jit(solution)/shard_map/reduce_scatter | solution.py:151
  (10 shorter events, 0.0 us)
Async XLA Ops:
  7.2 6.7 %copy-start.3 = (s32[1,1,8]{2,1,0:T(1,128)S(1)}, s32[1,1,8]{2,1,0:T(1,128)}, u32[]{:S(2)}) copy-start(s32[1,1,8]{2,1,0:T(1,128)} %param.19) | copy-start | bytes 100
  7.2 6.7 %copy-start.4 = (s32[1,1,8]{2,1,0:T(1,128)S(1)}, s32[1,1,8]{2,1,0:T(1,128)}, u32[]{:S(2)}) copy-start(s32[1,1,8]{2,1,0:T(1,128)} %param.18) | copy-start | bytes 100
  7.2 26.1 %all-gather.2.cloned.1.call-start = ((), (), s32[]{:S(2)}) async-start(), calls=%async_computation.2 | async-start | bytes 2129920 | tf_op jit(solution)/shard_map/all_gather | solution.py:119
  9.0 24.2 %copy-start = (bf16[104,2048]{1,0:T(8,128)(2,1)S(1)}, bf16[104,2048]{1,0:T(8,128)(2,1)}, u32[]{:S(2)}) copy-start(bf16[104,2048]{1,0:T(8,128)(2,1)} %sc_ref.1) | copy-start | bytes 1277956
  9.0 24.2 %copy-start.1 = (bf16[1,1,8,128,128]{4,3,2,1,0:T(8,128)(2,1)S(1)}, bf16[1,1,8,128,128]{4,3,2,1,0:T(8,128)(2,1)}, u32[]{:S(2)}) copy-start(bf16[1,1,8,128,128]{4,3,2,1,0:T(8,128)(2,1)} %param.21) | copy-start | bytes 786436
  9.0 24.2 %copy-start.2 = (bf16[16,2048]{1,0:T(8,128)(2,1)S(1)}, bf16[16,2048]{1,0:T(8,128)(2,1)}, u32[]{:S(2)}) copy-start(bf16[16,2048]{1,0:T(8,128)(2,1)} %kr_ref.1) | copy-start | bytes 196612
  9.1 146.4 %all-reduce.4.cloned.1.call-start = ((), (), s32[]{:S(2)}) async-start(), calls=%async_computation.5 | async-start | bytes 1114112 | tf_op jit(solution)/shard_map/psum | solution.py:152
  64.0 116.0 %reduce-scatter.3.cloned.1.call-start = ((), (), s32[]{:S(2)}) async-start(), calls=%async_computation.3 | async-start | bytes 655360 | tf_op jit(solution)/shard_map/reduce_scatter | solution.py:150
  64.7 145.3 %reduce-scatter.5.cloned.1.call-start = ((), (), s32[]{:S(2)}) async-start(), calls=%async_computation.4 | async-start | bytes 2129920 | tf_op jit(solution)/shard_map/reduce_scatter | solution.py:151
Sparse Core Ops, SparseCore 0:
  10.1 23.0 all-gather.1
  64.1 91.2 all-reduce.3
  158.3 21.6 reduce-scatter.2
  183.0 27.0 reduce-scatter.4
where the time goes:
time: 217 us
  waiting for transfers between devices  145 us (67%)
  Pallas kernels  29.9 us (14%)
  blocking collectives  17.4 us (8%)
  between operations  15.2 us (7%)
  local copies, waits for them, and re-layouts  8.54 us (4%)
    psum x1, waiting for transfers between devices, shards(): lax.psum(jnp.concatenate([gl, gr], 1), ('tp', 'dp', 'sub'))  90.1 us
    reduce_scatter x1, waiting for transfers between devices, shards(): lax.psum_scatter(ig, ('dp', 'sub'), scatter_dimension=0, tiled=True)[:own]  30.1 us
    pallas_call x1, Pallas kernels, shards(): pl.pallas_call(functools.partial(kernel, tokens, step_rows), in_specs=[sm...  29.9 us
    reduce_scatter x1, waiting for transfers between devices, shards(): lax.psum_scatter(out, 'tp', scatter_dimension=0, tiled=True)[:own]  21.2 us
    all_gather x1, blocking collectives, shards(): lax.all_gather(jnp.pad(out_grad, ((0, pad), (0, 0))), 'tp', axis=0, tiled...  17.4 us
  transfers between devices with their start and end apart: 4, of which 4 were waited for; matrix products, arithmetic and copies ran while one was open for 3% of the time, Pallas kernels for 0%

commit v1 on v0

v1 whole, which is shorter than its diff:
```python
import functools

import jax
import jax.numpy as jnp
from jax import lax
from jax.experimental import pallas as pl
from jax.experimental.pallas import tpu as pltpu
from jax.sharding import PartitionSpec as P

F32 = jnp.float32
BF16 = jnp.bfloat16
MESH = pl.DeviceIdType.MESH
LANES = 128


def dot(a, b, ca, cb):
    return lax.dot_general(a, b, (((ca,), (cb,)), ((), ())), preferred_element_type=F32)


def splits(blocks, pieces):
    pieces = min(pieces, blocks)
    cuts = [blocks * i // pieces for i in range(pieces + 1)]
    return [(cuts[i] * LANES, (cuts[i + 1] - cuts[i]) * LANES) for i in range(pieces)]


def window(blocks, parts):
    width = -(-blocks // parts)
    return width, blocks - width, max(parts - 1, 1)


def kernel(
    shape,
    rows_ref, cols_ref, count_ref, coef_ref, x_hbm, dy_hbm, kl_hbm, kr_hbm, sc_hbm, val_hbm, w_hbm,
    out_parts, ig_parts, go_ref, gl_hbm, gr_hbm, gs_hbm,
    wv, xl, xs, dl, ds, klv, krv, scb, scf, vals, mapv, maps,
    igb, igr, igs, ob, proj_s, gproj_s, mx, ux, glq, glr, glp, gla, glw, glall, grq, grr, grp, gra, grw, grall, glo, gro, gso,
    w_sem, in_sem, map_sem, own_sem, xring_s, xring_r, xsub_s, xsub_r, dy_s, dy_r,
    igsub_s, igsub_r, ig_s, ig_r, ig_own, out_s, out_r, out_own, mx_s, mx_r, ux_s, ux_r,
    gl1_s, gl1_r, gl2_s, gl2_r, gl3_s, gl3_r, gr1_s, gr1_r, gr2_s, gr2_r, gr3_s, gr3_r, res_sem,
):
    n_t, n_d, n_c, own, kc, fc, pieces = shape
    n_s = n_d * n_c
    t, d, c = lax.axis_index("tp"), lax.axis_index("dp"), lax.axis_index("sub")
    s = d * n_c + c
    tile_rows, tile_cols = w_hbm.shape
    slots, block = val_hbm.shape[0], val_hbm.shape[1]
    col_blocks, row_blocks = tile_cols // block, tile_rows // block
    nb, nf = tile_rows // kc, tile_cols // fc
    pad = xs.shape[1] // n_s
    quant = tile_rows // sc_hbm.shape[0]
    inv = 1.0 / (own * n_s)
    coef = coef_ref[0, 0]

    def joined(ref, start, count):
        return jnp.concatenate([ref[start + i] for i in range(count)], axis=1)

    def all_x():
        return joined(xs, 0, row_blocks)

    def all_dy():
        return joined(ds, 0, col_blocks)

    def plane(h):
        o = lax.rem(s + h, n_s)
        return o, {"dp": o // n_c, "sub": lax.rem(o, n_c)}

    def along(h):
        o = lax.rem(t + h, n_t)
        return o, {"tp": o}

    def remote(src, dst, send, recv, where):
        return pltpu.make_async_remote_copy(
            src_ref=src, dst_ref=dst, send_sem=send, recv_sem=recv, device_id=where, device_id_type=MESH
        )

    barrier = pltpu.get_barrier_semaphore()
    for h in range(1, n_t):
        pl.semaphore_signal(barrier, inc=1, device_id=along(h)[1], device_id_type=MESH)
    for h in range(1, n_s):
        pl.semaphore_signal(barrier, inc=1, device_id=plane(h)[1], device_id_type=MESH)

    locals_ = [
        pltpu.make_async_copy(sc_hbm, scb, in_sem.at[0]),
        pltpu.make_async_copy(val_hbm, vals.at[pl.ds(0, slots)], in_sem.at[1]),
        pltpu.make_async_copy(kl_hbm, klv, in_sem.at[2]),
        pltpu.make_async_copy(kr_hbm, krv, in_sem.at[3]),
    ]
    own_x = pltpu.make_async_copy(x_hbm, xl.at[s], own_sem.at[0])
    own_dy = pltpu.make_async_copy(dy_hbm, dl.at[t], own_sem.at[1])

    def fetch(i):
        part = pl.ds(pl.multiple_of(i * kc, kc), kc)
        return pltpu.make_async_copy(w_hbm.at[part], wv.at[part], w_sem.at[i])

    for copy in locals_[:2]:
        copy.start()
    fetch(0).start()
    own_x.start()
    own_dy.start()
    for copy in locals_[2:]:
        copy.start()

    pl.semaphore_wait(barrier, n_t - 1 + n_s - 1)

    right, left = lax.rem(d + 1, n_d), lax.rem(d + n_d - 1, n_d)
    bounds = splits(row_blocks, pieces)

    def ring(h, p):
        q = lax.rem(d - h + 1 + n_d, n_d)
        cols = pl.ds(*bounds[p])
        src = x_hbm.at[:, cols] if h == 1 else xl.at[q * n_c + c, :, cols]
        return remote(src, xl.at[q * n_c + c, :, cols], xring_s.at[h - 1, p], xring_r.at[h - 1, p], {"dp": right})

    def ring_in(h, p):
        q = lax.rem(d - h + n_d, n_d)
        cols = pl.ds(*bounds[p])
        ref = xl.at[q * n_c + c, :, cols]
        return remote(ref, ref, xring_s.at[h - 1, p], xring_r.at[h - 1, p], {"dp": left})

    def across(h, p, core):
        q = lax.rem(d - h + n_d, n_d)
        cols = pl.ds(*bounds[p])
        ref = xl.at[q * n_c + core, :, cols]
        src = x_hbm.at[:, cols] if h == 0 else ref
        return remote(src, ref, xsub_s.at[h, p], xsub_r.at[h, p], {"sub": 1 - c})

    for h in range(1, n_t):
        o, where = along(h)
        remote(dy_hbm, dl.at[t], dy_s.at[h - 1], dy_r.at[h - 1], where).start()
    for p in range(len(bounds)):
        ring(1, p).start()
    for p in range(len(bounds)):
        across(0, p, c).start()

    @pl.loop(1, nb)
    def _(i):
        fetch(i).start()

    ids = lax.broadcasted_iota(jnp.int32, mapv.shape, 0) * LANES + lax.broadcasted_iota(jnp.int32, mapv.shape, 1)
    table = jnp.full(mapv.shape, slots, jnp.int32)
    for m in range(slots):
        key = jnp.where(m < count_ref[0, 0], rows_ref[0, 0, m] * col_blocks + cols_ref[0, 0, m], -1)
        table = jnp.where(ids == key, m, table)
    mapv[...] = table
    to_map = pltpu.make_async_copy(mapv, maps, map_sem.at[0])
    to_map.start()
    vals[slots] = jnp.zeros((block, block), BF16)
    tail = own // 8 * 8
    for o in range(n_s):
        xs[:, o * pad + tail:(o + 1) * pad, :] = jnp.zeros((row_blocks, pad - tail, block), BF16)
    for o in range(n_t):
        ds[:, o * pad + tail:(o + 1) * pad, :] = jnp.zeros((col_blocks, pad - tail, block), BF16)
    locals_[0].wait()
    locals_[1].wait()
    scf[...] = scb[...].astype(F32)
    to_map.wait()

    group = 4 if col_blocks % 4 == 0 else 1
    chunk_blocks = kc // block
    marks = [row_blocks * (40 + 15 * p) // 100 for p in range(len(bounds))]

    def pass_on(h, p):
        ring_in(h, p).wait_recv()
        if h < n_d - 1:
            ring(h + 1, p).start()
        across(h, p, c).start()

    @pl.loop(0, row_blocks)
    def _(rb):
        @pl.when(lax.rem(rb, chunk_blocks) == 0)
        def _():
            fetch(rb // chunk_blocks).wait()

        for p in range(len(bounds)):
            @pl.when(rb == marks[p])
            def _():
                pass_on(1, p)

        for cb in range(0, col_blocks, group):
            cut = slice(cb * block, (cb + group) * block)
            delta = []
            for i in range(group):
                b = rb * col_blocks + cb + i
                delta.append(vals[maps[b // LANES, lax.rem(b, LANES)]])
            delta = jnp.concatenate(delta, axis=1)
            for q in range(block // quant):
                part = pl.ds(pl.multiple_of(rb * block + q * quant, quant), quant)
                sc = scf[pl.ds(rb * (block // quant) + q, 1), cut]
                sc = jnp.broadcast_to(sc, (16, group * block)).astype(BF16)
                sc = jnp.broadcast_to(sc[None], (quant // 16, 16, group * block)).reshape(quant, group * block)
                wv[part, cut] = wv[part, cut] * sc + delta[q * quant:(q + 1) * quant]

    own_dy.wait()
    for h in range(1, n_t):
        o = lax.rem(t - h + n_t, n_t)
        remote(dl.at[o], dl.at[o], dy_s.at[h - 1], dy_r.at[h - 1], {"tp": o}).wait_recv()
    for o in range(n_t):
        for b in range(col_blocks):
            ds[b, o * pad:o * pad + own, :] = dl[o, :, b * block:(b + 1) * block]
    locals_[2].wait()
    locals_[3].wait()

    gproj = dot(krv[...], all_dy(), 1, 1).astype(BF16).astype(F32)
    gproj_s[...] = gproj.T.astype(BF16)
    mx[s] = coef * gproj
    for h in range(1, n_s):
        o, where = plane(h)
        remote(mx.at[s], mx.at[s], mx_s.at[h - 1], mx_r.at[h - 1], where).start()

    def back(j):
        part = pl.ds(pl.multiple_of(j * kc, kc), kc)
        b = dot(all_dy(), wv[part, :], 1, 1)
        b += coef * dot(gproj_s[...], klv[:, part], 1, 0)
        b = b.astype(BF16)
        for o in range(n_s):
            igb[j, o % n_c, (o // n_c) * pad:(o // n_c + 1) * pad, :] = b[o * pad:(o + 1) * pad]

    def igsub(j):
        return remote(igb.at[j, 1 - c], igr.at[j], igsub_s.at[j], igsub_r.at[j], {"sub": 1 - c})

    def ig_out(j, h):
        o = lax.rem(d + h, n_d)
        part = pl.ds(pl.multiple_of(j * kc, kc), kc)
        src = igs.at[j, pl.ds(pl.multiple_of(o * pad, pad), pad)]
        if h == 0:
            return pltpu.make_async_copy(src, ig_parts.at[d, :, part], ig_own.at[j])
        return remote(src, ig_parts.at[d, :, part], ig_s.at[h - 1, j], ig_r.at[h - 1, j], {"dp": o})

    def ig_in(j, h):
        o = lax.rem(d - h + n_d, n_d)
        part = pl.ds(pl.multiple_of(j * kc, kc), kc)
        ref = ig_parts.at[o, :, part]
        return remote(ref, ref, ig_s.at[h - 1, j], ig_r.at[h - 1, j], {"dp": o})

    def combine(j):
        igsub(j).wait_recv()
        igs[j] = (igb[j, c].astype(F32) + igr[j].astype(F32)).astype(BF16)
        for h in range(n_d):
            ig_out(j, h).start()

    def step_back(j):
        back(j)
        igsub(j).start()

        @pl.when(j > 0)
        def _():
            combine(j - 1)

    def ob_out(f, h):
        o = lax.rem(t + h, n_t)
        part = pl.ds(pl.multiple_of(f * fc, fc), fc)
        src = ob.at[f, pl.ds(pl.multiple_of(o * pad, pad), pad)]
        if h == 0:
            return pltpu.make_async_copy(src, out_parts.at[t, :, part], out_own.at[f])
        return remote(src, out_parts.at[t, :, part], out_s.at[h - 1, f], out_r.at[h - 1, f], {"tp": o})

    def ob_in(f, h):
        o = lax.rem(t - h + n_t, n_t)
        part = pl.ds(pl.multiple_of(f * fc, fc), fc)
        ref = out_parts.at[o, :, part]
        return remote(ref, ref, out_s.at[h - 1, f], out_r.at[h - 1, f], {"tp": o})

    def step_forward(f):
        part = pl.ds(pl.multiple_of(f * fc, fc), fc)
        o = dot(all_x(), wv[:, part], 1, 0)
        o += coef * dot(proj_s[...], krv[:, part], 1, 0)
        ob[f] = o.astype(BF16)
        for h in range(n_t):
            ob_out(f, h).start()

    ks, ks_free, ks_den = window(row_blocks, n_s)
    kt, kt_free, kt_den = window(ks, n_t)
    rt, rt_free, rt_den = window(col_blocks, n_t)
    rs, rs_free, rs_den = window(rt, n_s)

    def cut_of(i, width, free, den):
        return pl.ds(pl.multiple_of((i * free // den) * LANES, LANES), width * LANES)

    def exchange(n, hop, src, dst, me, send, recv):
        out = []
        for h in range(1, n):
            o, where = hop(h)
            out.append(remote(src(o), dst.at[me], send.at[h - 1], recv.at[h - 1], where))
        return out

    def arrivals(n, hop, dst, send, recv):
        for h in range(1, n):
            o, where = hop(n - h)
            remote(dst.at[o], dst.at[o], send.at[h - 1], recv.at[h - 1], where).wait_recv()

    ex_mx = lambda: exchange(n_s, plane, lambda o: mx.at[s], mx, s, mx_s, mx_r)
    ex_ux = lambda: exchange(n_t, along, lambda o: ux.at[t], ux, t, ux_s, ux_r)
    ex_gl1 = lambda: exchange(n_t, along, lambda o: glq.at[:, cut_of(o, kt, kt_free, kt_den)], glr, t, gl1_s, gl1_r)
    ex_gr1 = lambda: exchange(n_s, plane, lambda o: grq.at[:, cut_of(o, rs, rs_free, rs_den)], grr, s, gr1_s, gr1_r)
    ex_gl2 = lambda: exchange(n_t, along, lambda o: glp, gla, t, gl2_s, gl2_r)
    ex_gr2 = lambda: exchange(n_s, plane, lambda o: grp, gra, s, gr2_s, gr2_r)
    ex_gl3 = lambda: exchange(n_s, plane, lambda o: glw, glall, s, gl3_s, gl3_r)
    ex_gr3 = lambda: exchange(n_t, along, lambda o: grw, grall, t, gr3_s, gr3_r)

    def stage0():
        arrivals(n_s, plane, mx, mx_s, mx_r)
        arrivals(n_t, along, ux, ux_s, ux_r)
        mixed = mx[0]
        for o in range(1, n_s):
            mixed += mx[o]
        used = ux[0]
        for o in range(1, n_t):
            used += ux[o]
        g = dot(mixed.astype(BF16), joined(xs, s * ks_free // ks_den, ks), 1, 0) * inv
        glq[...] = g.astype(BF16)
        glr[t] = glq[:, cut_of(t, kt, kt_free, kt_den)]
        grq[...] = dot(used.astype(BF16), joined(ds, t * rt_free // rt_den, rt), 1, 0) * inv
        grr[s] = grq[:, cut_of(s, rs, rs_free, rs_den)]
        for copy in ex_gl1() + ex_gr1():
            copy.start()

    def stage1():
        arrivals(n_t, along, glr, gl1_s, gl1_r)
        arrivals(n_s, plane, grr, gr1_s, gr1_r)
        g = glr[0].astype(F32)
        for o in range(1, n_t):
            g += glr[o].astype(F32)
        glp[...] = g.astype(BF16)
        gla[t] = g.astype(BF16)
        g = grr[0]
        for o in range(1, n_s):
            g += grr[o]
        grp[...] = g
        gra[s] = g
        for copy in ex_gl2() + ex_gr2():
            copy.start()

    def stage2():
        arrivals(n_t, along, gla, gl2_s, gl2_r)
        arrivals(n_s, plane, gra, gr2_s, gr2_r)
        for o in range(n_t):
            a = (o * kt_free // kt_den) * LANES
            glw[:, a:a + kt * LANES] = gla[o]
            glall[s, :, a:a + kt * LANES] = gla[o]
        for o in range(n_s):
            a = (o * rs_free // rs_den) * LANES
            grw[:, a:a + rs * LANES] = gra[o]
            grall[t, :, a:a + rs * LANES] = gra[o]
        for copy in ex_gl3() + ex_gr3():
            copy.start()

    gl_out = pltpu.make_async_copy(glo, gl_hbm, res_sem.at[0])
    gr_out = pltpu.make_async_copy(gro, gr_hbm, res_sem.at[1])
    gs_out = pltpu.make_async_copy(gso, gs_hbm, res_sem.at[2])

    def stage3():
        arrivals(n_s, plane, glall, gl3_s, gl3_r)
        arrivals(n_t, along, grall, gr3_s, gr3_r)
        for o in range(n_s):
            a = (o * ks_free // ks_den) * LANES
            glo[:, a:a + ks * LANES] = glall[o].astype(F32)
        for o in range(n_t):
            a = (o * rt_free // rt_den) * LANES
            gro[:, a:a + rt * LANES] = grall[o]
        gl_out.start()
        gr_out.start()

    per = (nb - 1) // nf
    first = nb - per * nf

    @pl.loop(0, first)
    def _(j):
        step_back(j)

    for h in range(2, n_d):
        for p in range(len(bounds)):
            pass_on(h, p)
    own_x.wait()
    for h in range(n_d):
        for p in range(len(bounds)):
            across(h, p, 1 - c).wait_recv()
    for o in range(n_s):
        for b in range(row_blocks):
            xs[b, o * pad:o * pad + own, :] = xl[o, :, b * block:(b + 1) * block]

    proj = dot(klv[...], all_x(), 1, 1).astype(BF16).astype(F32)
    proj_s[...] = proj.T.astype(BF16)
    ux[t] = coef * proj
    for copy in ex_ux():
        copy.start()
    go_ref[...] = (jnp.sum(proj * gproj) * inv).reshape(1, 1)

    @pl.loop(0, slots)
    def _(m):
        xr = xs[rows_ref[0, 0, m]]
        dc = ds[cols_ref[0, 0, m]]
        live = jnp.where(m < count_ref[0, 0], inv, 0.0)
        gso[m] = dot(xr, dc, 0, 0) * live

    gs_out.start()

    stages = [stage0, stage1, stage2]

    @pl.loop(0, nf)
    def _(f):
        @pl.loop(0, per)
        def _(i):
            step_back(first + f * per + i)

        for k in range(min(nf, len(stages))):
            @pl.when(f == k)
            def _():
                stages[k]()

        step_forward(f)

    combine(nb - 1)
    for k in range(nf, len(stages)):
        stages[k]()
    stage3()

    for copy in ex_mx() + ex_ux() + ex_gl1() + ex_gr1() + ex_gl2() + ex_gr2() + ex_gl3() + ex_gr3():
        copy.wait_send()
    for h in range(1, n_t):
        remote(dy_hbm, dl.at[t], dy_s.at[h - 1], dy_r.at[h - 1], along(h)[1]).wait_send()
    for p in range(len(bounds)):
        for h in range(1, n_d):
            ring(h, p).wait_send()
        for h in range(n_d):
            across(h, p, c).wait_send()

    @pl.loop(0, nb)
    def _(j):
        igsub(j).wait_send()
        ig_out(j, 0).wait()
        for h in range(1, n_d):
            ig_out(j, h).wait_send()
            ig_in(j, h).wait_recv()

    @pl.loop(0, nf)
    def _(f):
        ob_out(f, 0).wait()
        for h in range(1, n_t):
            ob_out(f, h).wait_send()
            ob_in(f, h).wait_recv()

    gl_out.wait()
    gr_out.wait()
    gs_out.wait()


def shards(
    hidden_in, out_grad, base_levels, base_scales, kron_outer, kron_left, kron_right,
    sparse_rows, sparse_cols, sparse_count, sparse_values,
):
    tile_rows, tile_cols = base_levels.shape
    slots, block = sparse_values.shape[2], sparse_values.shape[3]
    own = hidden_in.shape[0]
    pad = own + -own % 16
    rank = kron_left.shape[1]
    row_blocks, col_blocks = tile_rows // block, tile_cols // block
    n_d, n_c, n_t = lax.axis_size("dp"), lax.axis_size("sub"), lax.axis_size("tp")
    n_s = n_d * n_c
    full = n_s * pad
    kc = 4 * block if row_blocks % 4 == 0 else block
    fc = 4 * block if col_blocks % 4 == 0 else block
    nb, nf = tile_rows // kc, tile_cols // fc
    pieces = min(4, row_blocks)
    ks = window(row_blocks, n_s)[0]
    kt = window(ks, n_t)[0]
    rt = window(col_blocks, n_t)[0]
    rs = window(rt, n_s)[0]
    table_rows = -(-(row_blocks * col_blocks) // (8 * LANES)) * 8
    vmem = pl.BlockSpec(memory_space=pltpu.VMEM)
    smem = pl.BlockSpec(memory_space=pltpu.SMEM)
    any_ = pl.BlockSpec(memory_space=pl.ANY)
    dma = pltpu.SemaphoreType.DMA
    out_parts, ig_parts, go, gl, gr, gs = pl.pallas_call(
        functools.partial(kernel, (n_t, n_d, n_c, own, kc, fc, pieces)),
        in_specs=[smem] * 4 + [any_] * 7,
        out_specs=[any_, any_, vmem, any_, any_, any_],
        out_shape=[
            jax.ShapeDtypeStruct((n_t, pad, tile_cols), BF16),
            jax.ShapeDtypeStruct((n_d, pad, tile_rows), BF16),
            jax.ShapeDtypeStruct((1, 1), F32),
            jax.ShapeDtypeStruct((rank, tile_rows), F32),
            jax.ShapeDtypeStruct((rank, tile_cols), F32),
            jax.ShapeDtypeStruct((slots, block, block), F32),
        ],
        scratch_shapes=[
            pltpu.VMEM((tile_rows, tile_cols), BF16),
            pltpu.VMEM((n_s, own, tile_rows), BF16),
            pltpu.VMEM((row_blocks, full, block), BF16),
            pltpu.VMEM((n_t, own, tile_cols), BF16),
            pltpu.VMEM((col_blocks, full, block), BF16),
            pltpu.VMEM((rank, tile_rows), BF16),
            pltpu.VMEM((rank, tile_cols), BF16),
            pltpu.VMEM(base_scales.shape, BF16),
            pltpu.VMEM(base_scales.shape, F32),
            pltpu.VMEM((slots + 1, block, block), BF16),
            pltpu.VMEM((table_rows, LANES), jnp.int32),
            pltpu.SMEM((table_rows, LANES), jnp.int32),
            pltpu.VMEM((nb, n_c, n_d * pad, kc), BF16),
            pltpu.VMEM((nb, n_d * pad, kc), BF16),
            pltpu.VMEM((nb, n_d * pad, kc), BF16),
            pltpu.VMEM((nf, full, fc), BF16),
            pltpu.VMEM((full, rank), BF16),
            pltpu.VMEM((full, rank), BF16),
            pltpu.VMEM((n_s, rank, full), F32),
            pltpu.VMEM((n_t, rank, full), F32),
            pltpu.VMEM((rank, ks * LANES), BF16),
            pltpu.VMEM((n_t, rank, kt * LANES), BF16),
            pltpu.VMEM((rank, kt * LANES), BF16),
            pltpu.VMEM((n_t, rank, kt * LANES), BF16),
            pltpu.VMEM((rank, ks * LANES), BF16),
            pltpu.VMEM((n_s, rank, ks * LANES), BF16),
            pltpu.VMEM((rank, rt * LANES), F32),
            pltpu.VMEM((n_s, rank, rs * LANES), F32),
            pltpu.VMEM((rank, rs * LANES), F32),
            pltpu.VMEM((n_s, rank, rs * LANES), F32),
            pltpu.VMEM((rank, rt * LANES), F32),
            pltpu.VMEM((n_t, rank, rt * LANES), F32),
            pltpu.VMEM((rank, tile_rows), F32),
            pltpu.VMEM((rank, tile_cols), F32),
            pltpu.VMEM((slots, block, block), F32),
            dma((nb,)), dma((4,)), dma((1,)), dma((2,)),
            dma((n_d - 1, pieces)), dma((n_d - 1, pieces)), dma((n_d, pieces)), dma((n_d, pieces)),
            dma((n_t - 1,)), dma((n_t - 1,)),
            dma((nb,)), dma((nb,)), dma((n_d - 1, nb)), dma((n_d - 1, nb)), dma((nb,)),
            dma((n_t - 1, nf)), dma((n_t - 1, nf)), dma((nf,)),
            dma((n_s - 1,)), dma((n_s - 1,)), dma((n_t - 1,)), dma((n_t - 1,)),
            dma((n_t - 1,)), dma((n_t - 1,)), dma((n_t - 1,)), dma((n_t - 1,)), dma((n_s - 1,)), dma((n_s - 1,)),
            dma((n_s - 1,)), dma((n_s - 1,)), dma((n_s - 1,)), dma((n_s - 1,)), dma((n_t - 1,)), dma((n_t - 1,)),
            dma((3,)),
        ],
        compiler_params=pltpu.CompilerParams(
            vmem_limit_bytes=60 << 20, collective_id=0, has_side_effects=True
        ),
    )(
        sparse_rows, sparse_cols, sparse_count, kron_outer, hidden_in, out_grad, kron_left.T, kron_right,
        base_scales, sparse_values[0, 0], base_levels,
    )
    layer_out = jnp.sum(out_parts.astype(F32), axis=0).astype(BF16)[:own]
    input_grad = jnp.sum(ig_parts.astype(F32), axis=0).astype(BF16)[:own]
    return layer_out, input_grad, go, gl.T, gr, gs[None, None]


def solution(mesh):
    return jax.shard_map(
        shards,
        mesh=mesh,
        in_specs=(
            P(("grp", "dp", "sub"), "tp"),
            P(("grp", "tp"), ("dp", "sub")),
            P("tp", ("dp", "sub")),
            P("tp", ("dp", "sub")),
            P("tp", ("dp", "sub")),
            P(),
            P(),
            P("tp", ("dp", "sub"), None),
            P("tp", ("dp", "sub"), None),
            P("tp", ("dp", "sub")),
            P("tp", ("dp", "sub"), None, None, None),
        ),
        out_specs=(
            P(("grp", "tp"), ("dp", "sub")),
            P(("grp", "dp", "sub"), "tp"),
            P(("grp", "tp"), ("dp", "sub")),
            P("grp", None),
            P("grp", None),
            P(("grp", "tp"), ("dp", "sub"), None, None, None),
        ),
        check_vma=False,
    )
```

time: 217 us -> 60.2 us (0.28)
  waiting for transfers between devices: 145 us -> 0 us
  blocking collectives: 17.4 us -> 0 us
  Pallas kernels: 29.9 us -> 47 us
  between operations: 15.2 us -> 3.69 us
  local copies, waits for them, and re-layouts: 8.54 us -> 5.23 us
  other arithmetic: 0.95 us -> 3.98 us
    psum x1 -> x0, waiting for transfers between devices: 90.1 us -> none  [shards(): lax.psum(jnp.concatenate([gl, gr], 1), ('tp', 'dp', 'sub'))]
    reduce_scatter x2 -> x0, waiting for transfers between devices: 51.2 us -> none  [the longest x1 30.1 us: shards(): lax.psum_scatter(ig, ('dp', 'sub'), scatter_dimension=0, tiled=True)[:own]]
    all_gather x1 -> x0, blocking collectives: 17.4 us -> none  [shards(): lax.all_gather(jnp.pad(out_grad, ((0, pad), (0, 0))), 'tp', axis=0, tiled...]
    pallas_call x1, Pallas kernels: 29.9 us -> 47 us  [shards(): pl.pallas_call(functools.partial(kernel, (n_t, n_d, n_c, own, kc, fc, pie...]
    reduce_sum x1 -> x2, other arithmetic: 0.08 us -> 3.98 us  [the longest x1 2.17 us: shards(): input_grad = jnp.sum(ig_parts.astype(F32), axis=0).astype(BF16)[:own]]
    unnamed x11 -> x3, local copies, waits for them, and re-layouts: 2.47 us -> 5.23 us
    pad x2 -> x0, local copies, waits for them, and re-layouts: 2.71 us -> none  [the longest x1 1.8 us: shards(): jnp.pad(hidden_in, ((0, pad), (0, 0)))]
  transfers between devices with their start and end apart: 4 -> 0, of which waited for: 4 -> 0; matrix products, arithmetic and copies ran while one was open for 3% -> 0% of each run, Pallas kernels for 0% -> 0%
where the time goes in v1:
time: 60.2 us; the launch traced here: 59.9 us
  Pallas kernels  47 us (78%)
  local copies, waits for them, and re-layouts  5.23 us (9%)
  other arithmetic  3.98 us (7%)
  between operations  3.69 us (6%)
    pallas_call x1, Pallas kernels, shards(): pl.pallas_call(functools.partial(kernel, (n_t, n_d, n_c, own, kc, fc, pie...  47 us
    unnamed x3, local copies, waits for them, and re-layouts  5.23 us
    reduce_sum x1, other arithmetic, shards(): input_grad = jnp.sum(ig_parts.astype(F32), axis=0).astype(BF16)[:own]  2.17 us
    reduce_sum x1, other arithmetic, shards(): layer_out = jnp.sum(out_parts.astype(F32), axis=0).astype(BF16)[:own]  1.81 us

profile of v1, /device:TPU:0, one launch (start us, length us, event | category | flops | bytes accessed | tf_op | source)
XLA Modules:
  0.0 59.9 jit_solution(12130760683495048943)
XLA Ops:
  1.9 47.0 %shard_map.154 = (bf16[4,32,2048]{2,1,0:T(8,128)(2,1)}, bf16[2,32,6656]{2,1,0:T(8,128)(2,1)}, f32[1,1]{1,0:T(1,128)}, f32[16,6656]{1,0:T(8,128)}, f32[16,2048]{1,0:T(8,128)}, /*index=5*/f32[8,128,128]{2,1,0:T(8,128)}) custom-call(s32[1,1,8]{2,1,0:T(1,128)} %rows_ref.1, s32[1,1,8]{2,1,0:T(1,128)} %cols_ref.1, s32[1,1]{1,0:T(1,128)S(6)} %copy.22.count_ref, ...), custom_call_target="tpu_custom_call" | custom-call | tf_op jit(solution)/shard_map/pallas_call | solution.py:473
  48.9 1.8 %reduce_sum.24 = bf16[32,2048]{1,0:T(8,128)(2,1)} reduce(bf16[4,32,2048]{2,1,0:T(8,128)(2,1)} %get-tuple-element.12, bf16[]{:T(256)} %constant.3.clone.1), dimensions={0}, to_apply=%region_0.0 | reduce | flops 196608 | bytes 655362 | tf_op jit(solution)/shard_map/reduce_sum | solution.py:538
  50.7 2.2 %reduce_sum.25 = bf16[32,6656]{1,0:T(8,128)(2,1)} reduce(bf16[2,32,6656]{2,1,0:T(8,128)(2,1)} %get-tuple-element.13, bf16[]{:T(256)} %constant.3.clone.1), dimensions={0}, to_apply=%region_1.0 | reduce | flops 212992 | bytes 1277954 | tf_op jit(solution)/shard_map/reduce_sum | solution.py:539
  53.5 1.8 %copy.24 = f32[6656,16]{0,1:T(8,128)} copy(f32[6656,16]{0,1:T(8,128)} %bitcast.8) | data formatting | bytes 851968
  55.3 1.6 %copy.25 = f32[16,2048]{1,0:T(8,128)} copy(f32[16,2048]{1,0:T(8,128)} %get-tuple-element.28) | data formatting | bytes 262144
  56.9 1.9 %copy.26 = f32[1,1,8,128,128]{4,3,2,1,0:T(8,128)} copy(f32[1,1,8,128,128]{4,3,2,1,0:T(8,128)} %bitcast.6) | data formatting | bytes 1048576

commit v2 on v1

--- a/solution.py
+++ b/solution.py
@@ -94,11 +94,14 @@
 
     for copy in locals_[:2]:
         copy.start()
-    fetch(0).start()
     own_x.start()
     own_dy.start()
     for copy in locals_[2:]:
         copy.start()
+
+    @pl.loop(0, nb)
+    def _(i):
+        fetch(i).start()
 
     pl.semaphore_wait(barrier, n_t - 1 + n_s - 1)
 
@@ -131,10 +134,6 @@
         ring(1, p).start()
     for p in range(len(bounds)):
         across(0, p, c).start()
-
-    @pl.loop(1, nb)
-    def _(i):
-        fetch(i).start()
 
     ids = lax.broadcasted_iota(jnp.int32, mapv.shape, 0) * LANES + lax.broadcasted_iota(jnp.int32, mapv.shape, 1)
     table = jnp.full(mapv.shape, slots, jnp.int32)
@@ -190,23 +189,6 @@
                 sc = jnp.broadcast_to(sc[None], (quant // 16, 16, group * block)).reshape(quant, group * block)
                 wv[part, cut] = wv[part, cut] * sc + delta[q * quant:(q + 1) * quant]
 
-    own_dy.wait()
-    for h in range(1, n_t):
-        o = lax.rem(t - h + n_t, n_t)
-        remote(dl.at[o], dl.at[o], dy_s.at[h - 1], dy_r.at[h - 1], {"tp": o}).wait_recv()
-    for o in range(n_t):
-        for b in range(col_blocks):
-            ds[b, o * pad:o * pad + own, :] = dl[o, :, b * block:(b + 1) * block]
-    locals_[2].wait()
-    locals_[3].wait()
-
-    gproj = dot(krv[...], all_dy(), 1, 1).astype(BF16).astype(F32)
-    gproj_s[...] = gproj.T.astype(BF16)
-    mx[s] = coef * gproj
-    for h in range(1, n_s):
-        o, where = plane(h)
-        remote(mx.at[s], mx.at[s], mx_s.at[h - 1], mx_r.at[h - 1], where).start()
-
     def back(j):
         part = pl.ds(pl.multiple_of(j * kc, kc), kc)
         b = dot(all_dy(), wv[part, :], 1, 1)
@@ -360,16 +342,26 @@
         gl_out.start()
         gr_out.start()
 
-    per = (nb - 1) // nf
-    first = nb - per * nf
-
-    @pl.loop(0, first)
-    def _(j):
-        step_back(j)
-
     for h in range(2, n_d):
         for p in range(len(bounds)):
             pass_on(h, p)
+    own_dy.wait()
+    for h in range(1, n_t):
+        o = lax.rem(t - h + n_t, n_t)
+        remote(dl.at[o], dl.at[o], dy_s.at[h - 1], dy_r.at[h - 1], {"tp": o}).wait_recv()
+    for o in range(n_t):
+        for b in range(col_blocks):
+            ds[b, o * pad:o * pad + own, :] = dl[o, :, b * block:(b + 1) * block]
+    locals_[2].wait()
+    locals_[3].wait()
+
+    gproj = dot(krv[...], all_dy(), 1, 1).astype(BF16).astype(F32)
+    gproj_s[...] = gproj.T.astype(BF16)
+    mx[s] = coef * gproj
+    for h in range(1, n_s):
+        o, where = plane(h)
+        remote(mx.at[s], mx.at[s], mx_s.at[h - 1], mx_r.at[h - 1], where).start()
+
     own_x.wait()
     for h in range(n_d):
         for p in range(len(bounds)):
@@ -385,6 +377,30 @@
         copy.start()
     go_ref[...] = (jnp.sum(proj * gproj) * inv).reshape(1, 1)
 
+    per = nb // nf
+    stages = [stage0, stage1, stage2]
+
+    @pl.loop(0, nf)
+    def _(f):
+        for k in range(min(nf - 1, len(stages))):
+            @pl.when(f == k + 1)
+            def _():
+                stages[k]()
+
+        step_forward(f)
+
+        @pl.loop(0, per)
+        def _(i):
+            step_back(f * per + i)
+
+    @pl.loop(nf * per, nb)
+    def _(j):
+        step_back(j)
+
+    combine(nb - 1)
+    for k in range(nf - 1, len(stages)):
+        stages[k]()
+
     @pl.loop(0, slots)
     def _(m):
         xr = xs[rows_ref[0, 0, m]]
@@ -393,25 +409,6 @@
         gso[m] = dot(xr, dc, 0, 0) * live
 
     gs_out.start()
-
-    stages = [stage0, stage1, stage2]
-
-    @pl.loop(0, nf)
-    def _(f):
-        @pl.loop(0, per)
-        def _(i):
-            step_back(first + f * per + i)
-
-        for k in range(min(nf, len(stages))):
-            @pl.when(f == k)
-            def _():
-                stages[k]()
-
-        step_forward(f)
-
-    combine(nb - 1)
-    for k in range(nf, len(stages)):
-        stages[k]()
     stage3()
 
     for copy in ex_mx() + ex_ux() + ex_gl1() + ex_gr1() + ex_gl2() + ex_gr2() + ex_gl3() + ex_gr3():
@@ -442,6 +439,33 @@
     gl_out.wait()
     gr_out.wait()
     gs_out.wait()
+
+
+def finish(
+    out_parts, ig_parts, go_in, gl_in, gr_in, gs_in, out_hbm, ig_hbm, go_ref, gl_hbm, gr_hbm, gs_hbm,
+    op, ip, glv, grv, gsv, ov, iv, in_sem, out_sem,
+):
+    own = ov.shape[0]
+    passed = [(gs_in, gsv, gs_hbm), (gl_in, glv, gl_hbm), (gr_in, grv, gr_hbm)]
+    take = [pltpu.make_async_copy(ig_parts, ip, in_sem.at[0]), pltpu.make_async_copy(out_parts, op, in_sem.at[1])]
+    take += [pltpu.make_async_copy(a, v, in_sem.at[2 + i]) for i, (a, v, _) in enumerate(passed)]
+    give = [pltpu.make_async_copy(iv, ig_hbm, out_sem.at[0]), pltpu.make_async_copy(ov, out_hbm, out_sem.at[1])]
+    give += [pltpu.make_async_copy(v, o, out_sem.at[2 + i]) for i, (_, v, o) in enumerate(passed)]
+    for copy in take:
+        copy.start()
+    go_ref[...] = go_in[...]
+    for parts, total, i in ((ip, iv, 0), (op, ov, 1)):
+        take[i].wait()
+        acc = parts[0].astype(F32)
+        for o in range(1, parts.shape[0]):
+            acc += parts[o].astype(F32)
+        total[...] = acc.astype(BF16)[:own]
+        give[i].start()
+    for i in range(2, 5):
+        take[i].wait()
+        give[i].start()
+    for copy in give:
+        copy.wait()
 
 
 def shards(
@@ -535,8 +559,23 @@
         sparse_rows, sparse_cols, sparse_count, kron_outer, hidden_in, out_grad, kron_left.T, kron_right,
         base_scales, sparse_values[0, 0], base_levels,
     )
-    layer_out = jnp.sum(out_parts.astype(F32), axis=0).astype(BF16)[:own]
-    input_grad = jnp.sum(ig_parts.astype(F32), axis=0).astype(BF16)[:own]
+    parts = [out_parts, ig_parts, go, gl, gr, gs]
+    scratch = [pltpu.VMEM(p.shape, p.dtype) for p in parts]
+    results = [
+        jax.ShapeDtypeStruct((own, tile_cols), BF16), jax.ShapeDtypeStruct((own, tile_rows), BF16),
+        *[jax.ShapeDtypeStruct(p.shape, p.dtype) for p in parts[2:]],
+    ]
+    layer_out, input_grad, go, gl, gr, gs = pl.pallas_call(
+        finish,
+        in_specs=[any_, any_, vmem, any_, any_, any_],
+        out_specs=[any_, any_, vmem, any_, any_, any_],
+        out_shape=results,
+        scratch_shapes=[
+            scratch[0], scratch[1], scratch[3], scratch[4], scratch[5],
+            pltpu.VMEM((own, tile_cols), BF16), pltpu.VMEM((own, tile_rows), BF16), dma((5,)), dma((5,)),
+        ],
+        compiler_params=pltpu.CompilerParams(vmem_limit_bytes=60 << 20),
+    )(*parts)
     return layer_out, input_grad, go, gl.T, gr, gs[None, None]
 
 

time: 60.2 us -> 49.8 us (0.83)
  local copies, waits for them, and re-layouts: 5.23 us -> 0 us
  other arithmetic: 3.98 us -> 0 us
  between operations: 3.69 us -> 1.93 us
  Pallas kernels: 47 us -> 47.7 us
    unnamed x3 -> x0, local copies, waits for them, and re-layouts: 5.23 us -> none
    reduce_sum x2 -> x0, other arithmetic: 3.98 us -> none  [the longest x1 2.17 us: shards(): input_grad = jnp.sum(ig_parts.astype(F32), axis=0).astype(BF16)[:own]]
    pallas_call x0 -> x1, Pallas kernels: none -> 3.64 us  [shards(): pl.pallas_call(finish, in_specs=[any_, any_, vmem, any_, any_, any_], out...]
    pallas_call x1, Pallas kernels: 47 us -> 44.1 us  [shards(): pl.pallas_call(functools.partial(kernel, (n_t, n_d, n_c, own, kc, fc, pie...]
where the time goes in v2:
time: 49.8 us; the launch traced here: 49.6 us
  Pallas kernels  47.7 us (96%)
  between operations  1.93 us (4%)
    pallas_call x1, Pallas kernels, shards(): pl.pallas_call(functools.partial(kernel, (n_t, n_d, n_c, own, kc, fc, pie...  44.1 us
    pallas_call x1, Pallas kernels, shards(): pl.pallas_call(finish, in_specs=[any_, any_, vmem, any_, any_, any_], out...  3.64 us

profile of v2, /device:TPU:0, one launch (start us, length us, event | category | flops | bytes accessed | tf_op | source)
XLA Modules:
  0.0 49.6 jit_solution(16605132118934939427)
XLA Ops:
  1.9 44.1 %shard_map.154 = (bf16[4,32,2048]{2,1,0:T(8,128)(2,1)}, bf16[2,32,6656]{2,1,0:T(8,128)(2,1)}, f32[1,1]{1,0:T(1,128)}, f32[16,6656]{1,0:T(8,128)}, f32[16,2048]{1,0:T(8,128)}, /*index=5*/f32[8,128,128]{2,1,0:T(8,128)}) custom-call(s32[1,1,8]{2,1,0:T(1,128)} %rows_ref.1, s32[1,1,8]{2,1,0:T(1,128)} %cols_ref.1, s32[1,1]{1,0:T(1,128)S(6)} %copy.18.count_ref, ...), custom_call_target="tpu_custom_call" | custom-call | tf_op jit(solution)/shard_map/pallas_call | solution.py:497
  46.0 3.6 %shard_map.155 = (bf16[30,2048]{1,0:T(8,128)(2,1)}, bf16[30,6656]{1,0:T(8,128)(2,1)}, f32[1,1]{1,0:T(1,128)}, f32[16,6656]{1,0:T(8,128)}, f32[16,2048]{1,0:T(8,128)}, /*index=5*/f32[8,128,128]{2,1,0:T(8,128)}) custom-call(bf16[4,32,2048]{2,1,0:T(8,128)(2,1)} %get-tuple-element.18.out_parts, bf16[2,32,6656]{2,1,0:T(8,128)(2,1)} %get-tuple-element.19.ig_parts, ...), custom_call_target="tpu_custom_call" | custom-call | tf_op jit(solution)/shard_map/pallas_call | solution.py:568
